TPU v7x, 32 devices: a whole 2x2x4 slice. The times are simulated.
32 devices in a mesh: days: 2 (over y), chan: 4 (over z), tm: 2 (over x), freq: 2 (over core).
Axes of the slice: x: 2, y: 2, z: 4, core: 2. Of those that a mesh axis runs over, the one named last changes fastest.
Arguments:
- recording: bfloat16 [2048, 2048], P(('days', 'chan', 'freq'), 'tm'), parts along dimension 0, may hold values from -6 to 6
- trailing: bfloat16 [2048, 1024], P(('days', 'chan', 'freq')), parts along dimension 0, may hold values from -6 to 6
- whiten_filter: bfloat16 [1024, 64], P(('chan', 'freq')), may hold values from -0.75 to 0.75
- pair_list: int32 [8, 4], P(('days', 'chan')), parts along dimension 0, may hold values from -1 to 3, as said below
Outputs:
- cross_spectra: float32 [8, 4, 4, 2, 256, 256], P(('days', 'chan'), None, ('tm', 'freq')), parts along dimension 0
There are 2 independent parts, one for each index of `days`. A program takes and returns all parts, laid end to end along the dimension named above; an argument that names none is the same for every part. Nothing has to cross between parts.
Inputs may be any that keep to these rules, and one draw needn't show every extreme that they name: `pair_list`: row a lists in its first slots distinct blocks b with |b - a| <= 3, then -1 in the remaining slots; every row lists at least one block, and some row of every draw fills all 4 slots.
All inputs are finite; a program needn't handle non-finite values.
Results may differ from a plain program's by a relative error of at most 0.0046.
Values may be sent and summed in bfloat16 or wider, within the bound.
A program may use at most 64 MiB of HBM per device.

v0:
```python
import math

import jax
import jax.numpy as jnp
from jax import lax
from jax.sharding import PartitionSpec as P

FB = 512
REACH = 3
SLOTS = 4


def shifted(block, axis, distance):
    devices = range(lax.axis_size(axis))
    route = [(i - distance, i) for i in devices if i - distance in devices]
    return lax.ppermute(block, axis, route)


def extended(value, sides, width):
    for axis, dim in sides:
        size, length = (lax.axis_size(axis), value.shape[dim])
        up = [(i, (i + 1) % size) for i in range(size - 1)]
        down = [(j, i) for i, j in up]
        last = lax.slice_in_dim(value, length - width, length, axis=dim)
        initial = lax.slice_in_dim(value, 0, width, axis=dim)
        before = lax.ppermute(last, axis, up)
        after = lax.ppermute(initial, axis, down)
        value = jnp.concatenate([before, value, after], axis=dim)
    return value


def fourier_table(first_bin, bin_count, length):
    samples = jnp.arange(length, dtype=jnp.int32)[:, None]
    bin_index = first_bin + jnp.arange(bin_count, dtype=jnp.int32)[None, :]
    phase = samples * bin_index % length
    angle = 2.0 * math.pi / length * phase.astype(jnp.float32)
    taper = 0.5 - 0.5 * jnp.cos(
        2.0 * math.pi / length * jnp.arange(length, dtype=jnp.int32).astype(jnp.float32)
    )
    normaliser = 1.0 / math.sqrt(0.375 * length)
    cosine = (taper[:, None] * jnp.cos(angle) * normaliser).astype(jnp.bfloat16)
    sine_table = (-taper[:, None] * jnp.sin(angle) * normaliser).astype(jnp.bfloat16)
    return (cosine, sine_table)


def local(recording, trailing, whiten_filter, pair_list):
    local_rows, local_span = recording.shape
    hop_size = trailing.shape[1]
    window_size = 2 * hop_size
    segment_count = local_span // hop_size
    following = shifted(recording, "tm", -1)
    is_last = lax.axis_index("tm") == lax.axis_size("tm") - 1
    following = jnp.where(is_last, trailing, following)
    signal = jnp.concatenate([recording, following], axis=1)
    segments = jnp.stack([signal], axis=1)
    stacked_segments = segments.reshape(local_rows * segment_count, window_size)
    bin_step = min(256, FB)
    real_bins = []
    imag_bins = []
    for first_bin in range(0, FB, bin_step):
        cosine, sine_table = fourier_table(first_bin, bin_step, window_size)
        joined = jnp.concatenate([cosine, sine_table], axis=1)
        product = jnp.dot(stacked_segments, joined, preferred_element_type=jnp.float32).astype(
            jnp.bfloat16
        )
        real_bins.append(product[:, :bin_step])
        imag_bins.append(product[:, bin_step:])
    real_spec = jnp.concatenate(real_bins, axis=1)
    imag_spec = jnp.concatenate(imag_bins, axis=1)
    raw_spectra = jnp.stack([real_spec, imag_spec])
    tap_count = whiten_filter.shape[1]
    rim_width = tap_count // 2
    offset = (
        jnp.arange(local_rows + tap_count, dtype=jnp.int32)[None, :]
        - jnp.arange(local_rows, dtype=jnp.int32)[:, None]
    )
    inside = (offset >= 0) & (offset < tap_count)
    picked_weights = jnp.take_along_axis(whiten_filter, jnp.clip(offset, 0, tap_count - 1), axis=1)
    band_matrix = jnp.where(inside, picked_weights, jnp.zeros((), whiten_filter.dtype))
    padded = extended(raw_spectra, ((("chan", "freq"), 1),), rim_width)
    predicted = jnp.einsum("ij,ajk->aik", band_matrix, padded, preferred_element_type=jnp.float32)
    whitened = (raw_spectra.astype(jnp.float32) - predicted).astype(jnp.bfloat16)
    spectra = whitened.reshape(2, local_rows, segment_count, FB)
    tm_count = lax.axis_size("tm")
    freq_count = lax.axis_size("freq")
    pieces = lax.all_to_all(spectra[None], ("tm", "freq"), split_axis=4, concat_axis=0, tiled=True)
    band_width = pieces.shape[-1]
    pieces = pieces.reshape(tm_count, freq_count, 2, local_rows, segment_count, band_width)
    banded = pieces.transpose(2, 1, 3, 0, 4, 5).reshape(
        2, freq_count * local_rows, tm_count * segment_count, band_width
    )
    block_rows = banded.shape[1]
    own_block = banded.reshape(2, block_rows, -1)
    depth = own_block.shape[2]
    scaling = 1.0 / math.sqrt(depth)
    block_index = lax.axis_index("chan")
    slot_list = pair_list[0]
    nearby = []
    for distance in range(-REACH, REACH + 1):
        if distance == 0:
            nearby.append(own_block)
        else:
            nearby.append(shifted(own_block, "chan", -distance))
    stacked = jnp.stack(nearby)

    def fetch_partner(partner_index):
        return lax.dynamic_index_in_dim(
            stacked, partner_index - block_index + REACH, 0, keepdims=False
        )

    left_side = jnp.concatenate([own_block[0], own_block[1]], axis=1)
    flipped = jnp.concatenate([own_block[1], -own_block[0]], axis=1)
    contract = (((1,), (1,)), ((), ()))

    def one_slot(partner_index):
        partner = fetch_partner(partner_index)
        right_side = jnp.concatenate([partner[0], partner[1]], axis=1)
        real_part = (
            lax.dot_general(left_side, right_side, contract, preferred_element_type=jnp.float32)
            * scaling
        )
        imag_part = (
            lax.dot_general(flipped, right_side, contract, preferred_element_type=jnp.float32)
            * scaling
        )
        crossed = jnp.stack([real_part, imag_part])
        return jnp.where(partner_index >= 0, crossed, jnp.zeros((), jnp.float32))

    result = jnp.stack([one_slot(slot_list[slot_index]) for slot_index in range(SLOTS)])
    return result.reshape(1, SLOTS, 1, 2, block_rows, block_rows)


def solution(mesh):
    placed = (
        P(("days", "chan", "freq"), "tm"),
        P(("days", "chan", "freq"), None),
        P(("chan", "freq"), None),
        P(("days", "chan"), None),
    )
    return jax.shard_map(
        local,
        mesh=mesh,
        in_specs=placed,
        out_specs=P(("days", "chan"), None, ("tm", "freq"), None, None, None),
        check_vma=False,
    )
```

profile of v0, /device:TPU:0, one launch (start us, length us, event | category | flops | bytes accessed | tf_op | source)
XLA Modules:
  0.0 278.6 jit_solution(4303380736802716633)
XLA Ops:
  0.0 1.4 collective-permute-start
  1.6 19.2 %multiply_convert_fusion.2 = (bf16[2048,256]{1,0:T(8,128)(2,1)S(1)}, bf16[2048,256]{1,0:T(8,128)(2,1)S(1)}, bf16[2048,256]{1,0:T(8,128)(2,1)S(1)}, bf16[2048,256]{1,0:T(8,128)(2,1)}) fusion(f32[2048]{0:T(1024)S(1)} %fusion.64, s32[256]{0:T(256)S(1)} %iota_add_fusion, f32[2048]{0:T(1024)S(1)} %multiply_subtract_fusion), kind=kLoop, calls=%fused_computation.26 | loop fusion | flops 20971520 | bytes 4211712 | tf_op jit(solution)/shard_map/convert_element_type | solution.py:42
  20.7 1.0 broadcast_select_fusion
  21.7 1.8 fusion.34
  23.6 0.5 fusion.31
  24.1 2.4 collective-permute-start.1
  26.5 1.3 collective-permute-start.2
  28.0 195.9 %gather_fusion = bf16[24576]{0:T(1024)(128)(2,1)S(1)} fusion(bf16[128,64]{0,1:T(8,128)(2,1)S(1)} %copy-done, s32[24576]{0:T(1024)S(1)} %reshape.222), kind=kCustom, calls=%fused_computation | custom fusion | bytes 294912 | tf_op jit(solution)/shard_map/jit(take_along_axis)/gather | solution.py:78
  224.3 0.9 copy.28
  225.1 6.6 %all-to-all-start = ((bf16[1,2,128,1,512]{2,1,3,0,4:T(2,128)(2,1)}), bf16[1,2,128,1,512]{2,1,3,0,4:T(2,128)(2,1)S(1)}, u32[]{:S(2)}, u32[]{:S(2)}) async-start(bf16[1,2,128,1,512]{2,1,3,0,4:T(2,128)(2,1)} %copy.28), calls=%async_computation | async-start | bytes 524288 | tf_op jit(solution)/shard_map/all_to_all | solution.py:86
  231.7 0.7 fusion.84
  237.5 0.5 all-to-all-done
  238.3 0.3 copy.33
  238.8 5.6 %collective-permute-start.3 = (bf16[2,256,256]{2,1,0:T(8,128)(2,1)S(1)}, bf16[2,256,256]{2,1,0:T(8,128)(2,1)S(1)}, u32[]{:S(2)}, u32[]{:S(2)}) collective-permute-start(bf16[2,256,256]{2,1,0:T(8,128)(2,1)S(1)} %reshape_reshape.3), channel_id=1, source_target_pairs={{0,12},{1,13},{2,14},{3,15},{16,28},{17,29},{18,30},{19,31}} | collective-permute-start | bytes 786440 | tf_op jit(solution)/shard_map/ppermute | solution.py:16
  244.4 1.3 collective-permute-start.4
  245.7 2.5 collective-permute-start.5
  248.1 1.3 collective-permute-start.6
  249.4 1.3 collective-permute-start.7
  251.3 1.3 collective-permute-start.8
  252.7 4.0 %collective-permute-done.4 = bf16[2,256,256]{2,1,0:T(8,128)(2,1)S(1)} collective-permute-done((bf16[2,256,256]{2,1,0:T(8,128)(2,1)S(1)}, bf16[2,256,256]{2,1,0:T(8,128)(2,1)S(1)}, u32[]{:S(2)}, u32[]{:S(2)}) %collective-permute-start.4) | collective-permute-done | bytes 262176 | tf_op jit(solution)/shard_map/ppermute | solution.py:16
  256.7 5.0 %collective-permute-done.5 = bf16[2,256,256]{2,1,0:T(8,128)(2,1)S(1)} collective-permute-done((bf16[2,256,256]{2,1,0:T(8,128)(2,1)S(1)}, bf16[2,256,256]{2,1,0:T(8,128)(2,1)S(1)}, u32[]{:S(2)}, u32[]{:S(2)}) %collective-permute-start.5) | collective-permute-done | bytes 262176 | tf_op jit(solution)/shard_map/ppermute | solution.py:16
  261.8 12.8 %collective-permute-done.7 = bf16[2,256,256]{2,1,0:T(8,128)(2,1)S(1)} collective-permute-done((bf16[2,256,256]{2,1,0:T(8,128)(2,1)S(1)}, bf16[2,256,256]{2,1,0:T(8,128)(2,1)S(1)}, u32[]{:S(2)}, u32[]{:S(2)}) %collective-permute-start.7) | collective-permute-done | bytes 262176 | tf_op jit(solution)/shard_map/ppermute | solution.py:16
  275.8 0.3 fusion.26
  277.1 1.5 maximum_bitcast_fusion
  (55 shorter events, 3.8 us)
Async XLA Ops:
  0.0 28.0 %copy-start = (bf16[128,64]{0,1:T(8,128)(2,1)S(1)}, bf16[128,64]{0,1:T(8,128)(2,1)}, u32[]{:S(2)}) copy-start(bf16[128,64]{0,1:T(8,128)(2,1)} %param.6) | copy-start | bytes 49156
  0.0 20.7 %collective-permute-start = (bf16[128,1024]{1,0:T(8,128)(2,1)}, bf16[128,1024]{1,0:T(8,128)(2,1)}, u32[]{:S(2)}, u32[]{:S(2)}) collective-permute-start(bf16[128,1024]{1,0:T(8,128)(2,1)} %param.4), channel_id=1, source_target_pairs={{2,0},{3,1},{6,4},{7,5},{10,8},{11,9},{14,12},{15,13},{18,16},{19,... | collective-permute-start | bytes 786440 | tf_op jit(solution)/shard_map/ppermute | solution.py:16
  1.5 19.2 %copy-start.1 = (bf16[128,1024]{1,0:T(8,128)(2,1)S(1)}, bf16[128,1024]{1,0:T(8,128)(2,1)}, u32[]{:S(2)}) copy-start(bf16[128,1024]{1,0:T(8,128)(2,1)} %param.5) | copy-start | bytes 786436
  21.7 1.8 copy-start.3
  24.1 199.9 %collective-permute-start.1 = (bf16[2,32,512]{2,1,0:T(8,128)(2,1)S(1)}, bf16[2,32,512]{2,1,0:T(8,128)(2,1)S(1)}, u32[]{:S(2)}, u32[]{:S(2)}) collective-permute-start(bf16[2,32,512]{2,1,0:T(8,128)(2,1)S(1)} %get-tuple-element.15), channel_id=1, source_target_pairs={{0,1},{1,4},{4,5},{5,8},{8,9},{9,12},{12,13},{2,3},{3,6},{6,7},{7,... | collective-permute-start | bytes 196616 | tf_op jit(solution)/shard_map/ppermute | solution.py:26
  26.5 197.5 %collective-permute-start.2 = (bf16[2,32,512]{2,1,0:T(8,128)(2,1)S(1)}, bf16[2,32,512]{2,1,0:T(8,128)(2,1)S(1)}, u32[]{:S(2)}, u32[]{:S(2)}) collective-permute-start(bf16[2,32,512]{2,1,0:T(8,128)(2,1)S(1)} %get-tuple-element.16), channel_id=1, source_target_pairs={{1,0},{4,1},{5,4},{8,5},{9,8},{12,9},{13,12},{3,2},{6,3},{7,6},{10... | collective-permute-start | bytes 196616 | tf_op jit(solution)/shard_map/ppermute | solution.py:27
  223.9 7.8 %copy-start.2 = (s32[1,4]{1,0:T(1,128)S(1)}, s32[1,4]{1,0:T(1,128)}, u32[]{:S(2)}) copy-start(s32[1,4]{1,0:T(1,128)} %param.7) | copy-start | bytes 52
  225.1 12.9 %all-to-all-start = ((bf16[1,2,128,1,512]{2,1,3,0,4:T(2,128)(2,1)}), bf16[1,2,128,1,512]{2,1,3,0,4:T(2,128)(2,1)S(1)}, u32[]{:S(2)}, u32[]{:S(2)}) async-start(bf16[1,2,128,1,512]{2,1,3,0,4:T(2,128)(2,1)} %copy.28), calls=%async_computation | async-start | bytes 524288 | tf_op jit(solution)/shard_map/all_to_all | solution.py:86
  238.8 12.6 %collective-permute-start.3 = (bf16[2,256,256]{2,1,0:T(8,128)(2,1)S(1)}, bf16[2,256,256]{2,1,0:T(8,128)(2,1)S(1)}, u32[]{:S(2)}, u32[]{:S(2)}) collective-permute-start(bf16[2,256,256]{2,1,0:T(8,128)(2,1)S(1)} %reshape_reshape.3), channel_id=1, source_target_pairs={{0,12},{1,13},{2,14},{3,15},{16,28},{17,29},{18,30},{19,31}} | collective-permute-start | bytes 786440 | tf_op jit(solution)/shard_map/ppermute | solution.py:16
  244.4 12.4 %collective-permute-start.4 = (bf16[2,256,256]{2,1,0:T(8,128)(2,1)S(1)}, bf16[2,256,256]{2,1,0:T(8,128)(2,1)S(1)}, u32[]{:S(2)}, u32[]{:S(2)}) collective-permute-start(bf16[2,256,256]{2,1,0:T(8,128)(2,1)S(1)} %reshape_reshape.3), channel_id=1, source_target_pairs={{0,8},{4,12},{1,9},{5,13},{2,10},{6,14},{3,11},{7,15},{16,24},{20,... | collective-permute-start | bytes 786440 | tf_op jit(solution)/shard_map/ppermute | solution.py:16
  245.7 16.0 %collective-permute-start.5 = (bf16[2,256,256]{2,1,0:T(8,128)(2,1)S(1)}, bf16[2,256,256]{2,1,0:T(8,128)(2,1)S(1)}, u32[]{:S(2)}, u32[]{:S(2)}) collective-permute-start(bf16[2,256,256]{2,1,0:T(8,128)(2,1)S(1)} %reshape_reshape.3), channel_id=1, source_target_pairs={{0,4},{4,8},{8,12},{1,5},{5,9},{9,13},{2,6},{6,10},{10,14},{3,7},{... | collective-permute-start | bytes 786440 | tf_op jit(solution)/shard_map/ppermute | solution.py:16
  248.1 13.6 %collective-permute-start.6 = (bf16[2,256,256]{2,1,0:T(8,128)(2,1)S(1)}, bf16[2,256,256]{2,1,0:T(8,128)(2,1)S(1)}, u32[]{:S(2)}, u32[]{:S(2)}) collective-permute-start(bf16[2,256,256]{2,1,0:T(8,128)(2,1)S(1)} %reshape_reshape.3), channel_id=1, source_target_pairs={{4,0},{8,4},{12,8},{5,1},{9,5},{13,9},{6,2},{10,6},{14,10},{7,3},{... | collective-permute-start | bytes 786440 | tf_op jit(solution)/shard_map/ppermute | solution.py:16
  249.4 25.2 %collective-permute-start.7 = (bf16[2,256,256]{2,1,0:T(8,128)(2,1)S(1)}, bf16[2,256,256]{2,1,0:T(8,128)(2,1)S(1)}, u32[]{:S(2)}, u32[]{:S(2)}) collective-permute-start(bf16[2,256,256]{2,1,0:T(8,128)(2,1)S(1)} %reshape_reshape.3), channel_id=1, source_target_pairs={{8,0},{12,4},{9,1},{13,5},{10,2},{14,6},{11,3},{15,7},{24,16},{28,... | collective-permute-start | bytes 786440 | tf_op jit(solution)/shard_map/ppermute | solution.py:16
  251.3 23.3 %collective-permute-start.8 = (bf16[2,256,256]{2,1,0:T(8,128)(2,1)S(1)}, bf16[2,256,256]{2,1,0:T(8,128)(2,1)S(1)}, u32[]{:S(2)}, u32[]{:S(2)}) collective-permute-start(bf16[2,256,256]{2,1,0:T(8,128)(2,1)S(1)} %reshape_reshape.3), channel_id=1, source_target_pairs={{12,0},{13,1},{14,2},{15,3},{28,16},{29,17},{30,18},{31,19}} | collective-permute-start | bytes 786440 | tf_op jit(solution)/shard_map/ppermute | solution.py:16
where the time goes:
time: 279 us
  local copies, waits for them, and re-layouts  199 us (71%)
  starting transfers between devices  24.9 us (9%)
  waiting for transfers between devices  22.4 us (8%)
  other arithmetic  22 us (8%)
  between operations  5.63 us (2%)
  matrix products  4.59 us (2%)
    gather x3, local copies, waits for them, and re-layouts, local(): jnp.take_along_axis(whiten_filter, jnp.clip(offset, 0, tap_count - 1), ax...  196 us
    ppermute x7, waiting for transfers between devices, shifted(): return lax.ppermute(block, axis, route)  21.8 us
    convert_element_type x1, other arithmetic, fourier_table(): (-taper[:, None] * jnp.sin(angle) * normaliser).astype(jnp.bfloat16)  19.2 us
    ppermute x7, starting transfers between devices, shifted(): return lax.ppermute(block, axis, route)  14.7 us
    all_to_all x1, starting transfers between devices, local(): lax.all_to_all(spectra[None], ('tm', 'freq'), split_axis=4, concat_axis=0...  6.57 us
  transfers between devices with their start and end apart: 10, of which 4 were waited for; matrix products, arithmetic and copies ran while one was open for 78% of the time, Pallas kernels for 0%

commit v1 on v0

--- a/solution.py
+++ b/solution.py
@@ -1,8 +1,11 @@
+import functools
 import math
 
 import jax
 import jax.numpy as jnp
 from jax import lax
+from jax.experimental import pallas as pl
+from jax.experimental.pallas import tpu as pltpu
 from jax.sharding import PartitionSpec as P
 
 FB = 512
@@ -43,7 +46,7 @@
     return (cosine, sine_table)
 
 
-def local(recording, trailing, whiten_filter, pair_list):
+def general(recording, trailing, whiten_filter, pair_list):
     local_rows, local_span = recording.shape
     hop_size = trailing.shape[1]
     window_size = 2 * hop_size
@@ -70,13 +73,9 @@
     raw_spectra = jnp.stack([real_spec, imag_spec])
     tap_count = whiten_filter.shape[1]
     rim_width = tap_count // 2
-    offset = (
-        jnp.arange(local_rows + tap_count, dtype=jnp.int32)[None, :]
-        - jnp.arange(local_rows, dtype=jnp.int32)[:, None]
-    )
-    inside = (offset >= 0) & (offset < tap_count)
-    picked_weights = jnp.take_along_axis(whiten_filter, jnp.clip(offset, 0, tap_count - 1), axis=1)
-    band_matrix = jnp.where(inside, picked_weights, jnp.zeros((), whiten_filter.dtype))
+    reach_rows = local_rows + tap_count
+    skewed = jnp.pad(whiten_filter, ((0, 0), (0, local_rows + 1))).reshape(-1)
+    band_matrix = skewed[: local_rows * reach_rows].reshape(local_rows, reach_rows)
     padded = extended(raw_spectra, ((("chan", "freq"), 1),), rim_width)
     predicted = jnp.einsum("ij,ajk->aik", band_matrix, padded, preferred_element_type=jnp.float32)
     whitened = (raw_spectra.astype(jnp.float32) - predicted).astype(jnp.bfloat16)
@@ -130,6 +129,380 @@
     return result.reshape(1, SLOTS, 1, 2, block_rows, block_rows)
 
 
+MESH = pl.DeviceIdType.MESH
+TIERS = ((64, 128), (0, 64), (192, 64))
+PIECES = 4
+STEP = 32
+TILE = 64
+
+
+def spectra_kernel(
+    chan_count,
+    window_slots,
+    rec_ref,
+    trail_ref,
+    filt_ref,
+    gathered,
+    samples,
+    filters,
+    table,
+    coarse,
+    raw,
+    span_sems,
+    core_sems,
+    pass_sems,
+    rim_sems,
+    block_sems,
+):
+    me = lax.axis_index("chan")
+    tm = lax.axis_index("tm")
+    core = lax.axis_index("freq")
+    rows, hop = rec_ref.shape
+    window = 2 * hop
+    width = table.shape[1] // 2
+    block_rows = 2 * rows
+    rim = filt_ref.shape[1] // 2
+    has_left = me > 0
+    has_right = me < chan_count - 1
+    other_tm = {"tm": 1 - tm}
+    other_core = {"freq": 1 - core}
+    left = {"chan": me - 1}
+    right = {"chan": me + 1}
+
+    def remote(source, target, sems, index, device):
+        return pltpu.make_async_remote_copy(
+            src_ref=source,
+            dst_ref=target,
+            send_sem=sems.at[(0,) + index],
+            recv_sem=sems.at[(1,) + index],
+            device_id=device,
+            device_id_type=MESH,
+        )
+
+    barrier = pltpu.get_barrier_semaphore()
+    pl.semaphore_signal(barrier, inc=1, device_id=other_tm, device_id_type=MESH)
+    pl.semaphore_signal(barrier, inc=1, device_id=other_core, device_id_type=MESH)
+
+    @pl.when(has_left)
+    def _():
+        pl.semaphore_signal(barrier, inc=1, device_id=left, device_id_type=MESH)
+
+    @pl.when(has_right)
+    def _():
+        pl.semaphore_signal(barrier, inc=1, device_id=right, device_id_type=MESH)
+
+    pl.semaphore_wait(barrier, 2 + has_left.astype(jnp.int32) + has_right.astype(jnp.int32))
+
+    piece = rows // PIECES
+
+    def piece_rows(index):
+        return pl.ds(index * piece, piece)
+
+    span_copies = [
+        remote(
+            rec_ref.at[piece_rows(p)],
+            samples.at[tm, core, piece_rows(p)],
+            span_sems,
+            (p,),
+            other_tm,
+        )
+        for p in range(PIECES)
+    ]
+    for copy in span_copies:
+        copy.start()
+    core_copies = [
+        remote(rec_ref, samples.at[tm, core], core_sems, (0,), other_core),
+        remote(trail_ref, samples.at[2, core], core_sems, (1,), other_core),
+        remote(filt_ref, filters.at[core], core_sems, (2,), other_core),
+    ]
+    for copy in core_copies:
+        copy.start()
+
+    samples[tm, core] = rec_ref[...]
+    samples[2, core] = trail_ref[...]
+    filters[core] = filt_ref[...]
+
+    first_bin = (tm * 2 + core) * width
+    unit = 2.0 * math.pi / window
+    bins = first_bin + lax.broadcasted_iota(jnp.int32, (1, width), 1)
+
+    def angles(count, scale, factor):
+        steps = scale * lax.broadcasted_iota(jnp.int32, (count, width), 0)
+        return unit * jnp.bitwise_and(steps * factor, window - 1).astype(jnp.float32)
+
+    parts = window // STEP
+    coarse_angle = angles(parts, STEP, bins)
+    coarse_turn = angles(parts, STEP, 1)
+    coarse[0] = jnp.cos(coarse_angle)
+    coarse[1] = jnp.sin(coarse_angle)
+    coarse[2] = jnp.cos(coarse_turn)
+    coarse[3] = jnp.sin(coarse_turn)
+    fine_angle = angles(STEP, 1, bins)
+    fine_turn = angles(STEP, 1, 1)
+    fine_cos, fine_sin = jnp.cos(fine_angle), jnp.sin(fine_angle)
+    turn_cos, turn_sin = jnp.cos(fine_turn), jnp.sin(fine_turn)
+    normaliser = 1.0 / math.sqrt(0.375 * window)
+
+    def fill(part, carry):
+        c, s, tc, ts = (coarse[k, pl.ds(part, 1), :] for k in range(4))
+        taper = (0.5 - 0.5 * (tc * turn_cos - ts * turn_sin)) * normaliser
+        at = pl.ds(pl.multiple_of(part * STEP, STEP), STEP)
+        table[at, :width] = (taper * (c * fine_cos - s * fine_sin)).astype(jnp.bfloat16)
+        table[at, width:] = (-taper * (s * fine_cos + c * fine_sin)).astype(jnp.bfloat16)
+        return carry
+
+    lax.fori_loop(0, parts, fill, 0)
+
+    @pl.when(jnp.logical_not(has_left))
+    def _():
+        raw[0:rim] = jnp.zeros((rim, raw.shape[1]), raw.dtype)
+
+    @pl.when(jnp.logical_not(has_right))
+    def _():
+        raw[rim + block_rows : 2 * rim + block_rows] = jnp.zeros((rim, raw.shape[1]), raw.dtype)
+
+    pass_copies = [
+        remote(
+            samples.at[1 - tm, core, piece_rows(p)],
+            samples.at[1 - tm, core, piece_rows(p)],
+            pass_sems,
+            (p,),
+            other_core,
+        )
+        for p in range(PIECES)
+    ]
+    arriving = [
+        remote(
+            rec_ref.at[piece_rows(p)],
+            samples.at[1 - tm, core, piece_rows(p)],
+            span_sems,
+            (p,),
+            other_tm,
+        )
+        for p in range(PIECES)
+    ]
+    for p in range(PIECES):
+        arriving[p].wait_recv()
+        pass_copies[p].start()
+
+    def transform(half):
+        pair = samples[0:2, half].reshape(2 * rows, hop)
+        later = samples[1:3, half].reshape(2 * rows, hop)
+        product = jnp.dot(pair, table[:hop], preferred_element_type=jnp.float32) + jnp.dot(
+            later, table[hop:], preferred_element_type=jnp.float32
+        )
+        product = product.astype(jnp.bfloat16)
+        at = pl.ds(pl.multiple_of(rim + half * rows, rim), rows)
+        raw[at, 0:width] = product[:rows, :width]
+        raw[at, width : 2 * width] = product[rows:, :width]
+        raw[at, 2 * width : 3 * width] = product[:rows, width:]
+        raw[at, 3 * width : 4 * width] = product[rows:, width:]
+
+    transform(core)
+    other = 1 - core
+    remote(rec_ref, samples.at[tm, other], core_sems, (0,), other_core).wait_recv()
+    remote(trail_ref, samples.at[2, other], core_sems, (1,), other_core).wait_recv()
+    remote(filt_ref, filters.at[other], core_sems, (2,), other_core).wait_recv()
+    for p in range(PIECES):
+        remote(
+            samples.at[1 - tm, core, piece_rows(p)],
+            samples.at[1 - tm, other, piece_rows(p)],
+            pass_sems,
+            (p,),
+            other_core,
+        ).wait_recv()
+    transform(other)
+
+    to_right = remote(raw.at[block_rows : block_rows + rim], raw.at[0:rim], rim_sems, (0,), right)
+    to_left = remote(
+        raw.at[rim : 2 * rim],
+        raw.at[rim + block_rows : 2 * rim + block_rows],
+        rim_sems,
+        (1,),
+        left,
+    )
+
+    @pl.when(has_right)
+    def _():
+        to_right.start()
+
+    @pl.when(has_left)
+    def _():
+        to_left.start()
+
+    own_slot = lax.rem(me, window_slots)
+
+    def whiten(tile):
+        weights = filters[tile * TILE // rows, tile * TILE % rows : tile * TILE % rows + TILE]
+        wide = jnp.concatenate(
+            [weights.astype(jnp.float32), jnp.zeros((TILE, TILE), jnp.float32)], axis=1
+        )
+        band = pltpu.roll(wide, 0, 1, stride=1, stride_axis=0).astype(jnp.bfloat16)
+        near = raw[tile * TILE : tile * TILE + 2 * TILE]
+        predicted = jnp.dot(band, near, preferred_element_type=jnp.float32)
+        mine = raw[rim + tile * TILE : rim + tile * TILE + TILE].astype(jnp.float32)
+        gathered[own_slot, tile * TILE : tile * TILE + TILE] = (mine - predicted).astype(
+            jnp.bfloat16
+        )
+
+    def block_copy(direction, distance, tier):
+        start, count = TIERS[tier]
+        source = me - distance if direction == 0 else me + distance
+        slot = lax.rem(jnp.clip(source, 0, chan_count - 1), window_slots)
+        at = gathered.at[slot, pl.ds(start, count)]
+        return remote(
+            at, at, block_sems, (direction, distance, tier), right if direction == 0 else left
+        )
+
+    def landed(direction, distance, tier):
+        start, count = TIERS[tier]
+        source = me - distance if direction == 0 else me + distance
+        slot = lax.rem(jnp.clip(source, 0, chan_count - 1), window_slots)
+        at = gathered.at[slot, pl.ds(start, count)]
+        return remote(
+            at, at, block_sems, (direction, distance - 1, tier), right if direction == 0 else left
+        )
+
+    ahead = (has_right, has_left)
+
+    def send_own(tier):
+        for direction in range(2):
+
+            @pl.when(ahead[direction])
+            def _():
+                block_copy(direction, 0, tier).start()
+
+    whiten(1)
+    whiten(2)
+    send_own(0)
+
+    @pl.when(has_left)
+    def _():
+        remote(raw.at[0:rim], raw.at[0:rim], rim_sems, (0,), right).wait_recv()
+
+    whiten(0)
+    send_own(1)
+
+    @pl.when(has_right)
+    def _():
+        at = raw.at[rim + block_rows : 2 * rim + block_rows]
+        remote(at, at, rim_sems, (1,), left).wait_recv()
+
+    whiten(3)
+    send_own(2)
+
+    furthest = min(REACH, chan_count - 1)
+
+    def exists(direction, distance):
+        return me - distance >= 0 if direction == 0 else me + distance < chan_count
+
+    for distance in range(1, furthest + 1):
+        for tier in range(len(TIERS)):
+            for direction in range(2):
+
+                @pl.when(exists(direction, distance))
+                def _():
+                    landed(direction, distance, tier).wait_recv()
+
+                if distance < furthest:
+
+                    @pl.when(jnp.logical_and(exists(direction, distance), ahead[direction]))
+                    def _():
+                        block_copy(direction, distance, tier).start()
+
+    for copy in span_copies + core_copies + pass_copies:
+        copy.wait_send()
+
+    @pl.when(has_right)
+    def _():
+        to_right.wait_send()
+
+    @pl.when(has_left)
+    def _():
+        to_left.wait_send()
+
+    for distance in range(furthest):
+        for tier in range(len(TIERS)):
+            for direction in range(2):
+
+                @pl.when(jnp.logical_and(exists(direction, distance), ahead[direction]))
+                def _():
+                    block_copy(direction, distance, tier).wait_send()
+
+
+def cross_kernel(window_slots, scaling, pairs_ref, gathered, out_ref):
+    slot = pl.program_id(0)
+    me = lax.rem(lax.axis_index("chan"), window_slots)
+    partner = pairs_ref[0, slot]
+    half = gathered.shape[2] // 2
+    contract = (((1,), (1,)), ((), ()))
+
+    @pl.when(partner >= 0)
+    def _():
+        own = gathered[me]
+        right_side = gathered[lax.rem(jnp.maximum(partner, 0), window_slots)]
+        turned = jnp.concatenate([own[:, half:], -own[:, :half]], axis=1)
+        real = lax.dot_general(own, right_side, contract, preferred_element_type=jnp.float32)
+        out_ref[0, 0, 0, 0] = real * scaling
+        imag = lax.dot_general(turned, right_side, contract, preferred_element_type=jnp.float32)
+        out_ref[0, 0, 0, 1] = imag * scaling
+
+    @pl.when(partner < 0)
+    def _():
+        out_ref[...] = jnp.zeros_like(out_ref)
+
+
+def fused(recording, trailing, whiten_filter, pair_list):
+    rows, hop = recording.shape
+    chan_count = lax.axis_size("chan")
+    window_slots = min(chan_count, 2 * REACH + 1)
+    taps = whiten_filter.shape[1]
+    width = FB // (lax.axis_size("tm") * lax.axis_size("freq"))
+    block_rows = 2 * rows
+    depth = 2 * width
+    furthest = min(REACH, chan_count - 1)
+    vmem = pl.BlockSpec(memory_space=pltpu.VMEM)
+    gathered = pl.pallas_call(
+        functools.partial(spectra_kernel, chan_count, window_slots),
+        out_shape=jax.ShapeDtypeStruct((window_slots, block_rows, 2 * depth), jnp.bfloat16),
+        in_specs=[vmem] * 3,
+        out_specs=vmem,
+        scratch_shapes=[
+            pltpu.VMEM((3, 2, rows, hop), jnp.bfloat16),
+            pltpu.VMEM((2, rows, taps), jnp.bfloat16),
+            pltpu.VMEM((2 * hop, 2 * width), jnp.bfloat16),
+            pltpu.VMEM((4, 2 * hop // STEP, width), jnp.float32),
+            pltpu.VMEM((block_rows + taps, 2 * depth), jnp.bfloat16),
+            pltpu.SemaphoreType.DMA((2, PIECES)),
+            pltpu.SemaphoreType.DMA((2, 3)),
+            pltpu.SemaphoreType.DMA((2, PIECES)),
+            pltpu.SemaphoreType.DMA((2, 2)),
+            pltpu.SemaphoreType.DMA((2, 2, furthest, len(TIERS))),
+        ],
+        compiler_params=pltpu.CompilerParams(collective_id=0, has_side_effects=True),
+    )(recording, trailing, whiten_filter)
+    return pl.pallas_call(
+        functools.partial(cross_kernel, window_slots, 1.0 / math.sqrt(depth)),
+        out_shape=jax.ShapeDtypeStruct((1, SLOTS, 1, 2, block_rows, block_rows), jnp.float32),
+        grid_spec=pltpu.PrefetchScalarGridSpec(
+            num_scalar_prefetch=1,
+            grid=(SLOTS,),
+            in_specs=[vmem],
+            out_specs=pl.BlockSpec(
+                (1, 1, 1, 2, block_rows, block_rows), lambda slot, pairs: (0, slot, 0, 0, 0, 0)
+            ),
+        ),
+    )(pair_list, gathered)
+
+
+def local(recording, trailing, whiten_filter, pair_list):
+    shapes = (recording.shape, trailing.shape, whiten_filter.shape)
+    counts = (lax.axis_size("tm"), lax.axis_size("freq"))
+    if shapes == ((128, 1024), (128, 1024), (128, 64)) and counts == (2, 2):
+        return fused(recording, trailing, whiten_filter, pair_list)
+    return general(recording, trailing, whiten_filter, pair_list)
+
+
 def solution(mesh):
     placed = (
         P(("days", "chan", "freq"), "tm"),

time: 279 us -> 41.1 us (0.15)
  local copies, waits for them, and re-layouts: 199 us -> 1.43 us
  Pallas kernels: 0 us -> 39.7 us
  starting transfers between devices: 24.9 us -> 0 us
  waiting for transfers between devices: 22.4 us -> 0 us
  other arithmetic: 22 us -> 0 us
  between operations: 5.63 us -> 0.01 us
  matrix products: 4.59 us -> 0 us
    gather x3 -> x0, local copies, waits for them, and re-layouts: 196 us -> none  [local(): jnp.take_along_axis(whiten_filter, jnp.clip(offset, 0, tap_count - 1), ax...]
    pallas_call x0 -> x2, Pallas kernels: none -> 39.7 us  [the longest x1 35.1 us: fused(): pl.pallas_call(functools.partial(spectra_kernel, chan_count, window_slots...]
    ppermute x9 -> x0, waiting for transfers between devices: 21.8 us -> none  [the longest x7 21.8 us: shifted(): return lax.ppermute(block, axis, route)]
    convert_element_type x1 -> x0, other arithmetic: 19.2 us -> none  [fourier_table(): (-taper[:, None] * jnp.sin(angle) * normaliser).astype(jnp.bfloat16)]
    ppermute x9 -> x0, starting transfers between devices: 18.4 us -> none  [the longest x7 14.7 us: shifted(): return lax.ppermute(block, axis, route)]
    all_to_all x1 -> x0, starting transfers between devices: 6.57 us -> none  [local(): lax.all_to_all(spectra[None], ('tm', 'freq'), split_axis=4, concat_axis=0...]
    dot_general x11 -> x0, matrix products: 4.59 us -> none  [the longest x2 2.26 us: local(): jnp.dot(stacked_segments, joined, preferred_element_type=jnp.float32)]
  transfers between devices with their start and end apart: 10 -> 0, of which waited for: 4 -> 0; matrix products, arithmetic and copies ran while one was open for 78% -> 0% of each run, Pallas kernels for 0% -> 0%
where the time goes in v1:
time: 41.1 us
  Pallas kernels  39.7 us (97%)
  local copies, waits for them, and re-layouts  1.43 us (3%)
    pallas_call x1, Pallas kernels, fused(): pl.pallas_call(functools.partial(spectra_kernel, chan_count, window_slots...  35.1 us
    pallas_call x1, Pallas kernels, fused(): pl.pallas_call(functools.partial(cross_kernel, window_slots, 1.0 / math.s...  4.56 us
    unnamed x1, local copies, waits for them, and re-layouts  1.43 us

profile of v1, /device:TPU:0, one launch (start us, length us, event | category | flops | bytes accessed | tf_op | source)
XLA Modules:
  0.0 41.1 jit_solution(136070471077718254)
XLA Ops:
  0.0 1.4 %copy.5.filt_ref = bf16[128,64]{1,0:T(8,128)(2,1)} copy(bf16[128,64]{0,1:T(8,128)(2,1)} %param.6) | data formatting | bytes 32768 | tf_op args[2]
  1.4 35.1 %shard_map.46.gathered = bf16[4,256,512]{2,1,0:T(8,128)(2,1)} custom-call(bf16[128,1024]{1,0:T(8,128)(2,1)} %rec_ref.1, bf16[128,1024]{1,0:T(8,128)(2,1)} %trail_ref.1, bf16[128,64]{1,0:T(8,128)(2,1)} %copy.5.filt_ref), custom_call_target="tpu_custom_call" | custom-call | tf_op jit(solution)/shard_map/pallas_call | solution.py:465
  36.5 4.6 %shard_map.47 = f32[1,4,1,2,256,256]{5,4,3,2,1,0:T(8,128)} custom-call(s32[1,4]{1,0:T(1,128)} %pairs_ref.1, bf16[4,256,512]{2,1,0:T(8,128)(2,1)} %shard_map.46.gathered), custom_call_target="tpu_custom_call" | custom-call | tf_op jit(solution)/shard_map/pallas_call | solution.py:484

commit v2 on v1

--- a/solution.py
+++ b/solution.py
@@ -130,24 +130,26 @@
 
 
 MESH = pl.DeviceIdType.MESH
-TIERS = ((64, 128), (0, 64), (192, 64))
 PIECES = 4
 STEP = 32
-TILE = 64
 
 
 def spectra_kernel(
     chan_count,
     window_slots,
+    scaling,
     rec_ref,
     trail_ref,
     filt_ref,
-    gathered,
+    crossed,
     samples,
     filters,
+    bands,
     table,
     coarse,
     raw,
+    gathered,
+    local_sems,
     span_sems,
     core_sems,
     pass_sems,
@@ -161,9 +163,12 @@
     window = 2 * hop
     width = table.shape[1] // 2
     block_rows = 2 * rows
-    rim = filt_ref.shape[1] // 2
+    taps = filt_ref.shape[0]
+    rim = taps // 2
+    piece = rows // PIECES
     has_left = me > 0
     has_right = me < chan_count - 1
+    other = 1 - core
     other_tm = {"tm": 1 - tm}
     other_core = {"freq": 1 - core}
     left = {"chan": me - 1}
@@ -179,6 +184,9 @@
             device_id_type=MESH,
         )
 
+    def half(which):
+        return pl.ds(pl.multiple_of(which * rows, rows), rows)
+
     barrier = pltpu.get_barrier_semaphore()
     pl.semaphore_signal(barrier, inc=1, device_id=other_tm, device_id_type=MESH)
     pl.semaphore_signal(barrier, inc=1, device_id=other_core, device_id_type=MESH)
@@ -191,17 +199,29 @@
     def _():
         pl.semaphore_signal(barrier, inc=1, device_id=right, device_id_type=MESH)
 
+    own_copies = [
+        pltpu.make_async_copy(rec_ref, samples.at[tm, half(core)], local_sems.at[0]),
+        pltpu.make_async_copy(trail_ref, samples.at[2, half(core)], local_sems.at[1]),
+        pltpu.make_async_copy(filt_ref, filters.at[core], local_sems.at[2]),
+    ]
+    for copy in own_copies:
+        copy.start()
+
     pl.semaphore_wait(barrier, 2 + has_left.astype(jnp.int32) + has_right.astype(jnp.int32))
 
-    piece = rows // PIECES
-
-    def piece_rows(index):
-        return pl.ds(index * piece, piece)
+    def piece_start(which, step):
+        return pl.multiple_of(
+            (1 - which) * (PIECES - 1 - step) * piece + which * step * piece, piece
+        )
+
+    def piece_in_block(which, step):
+        start = which * rows + piece_start(which, step)
+        return pl.ds(pl.multiple_of(start, piece), piece)
 
     span_copies = [
         remote(
-            rec_ref.at[piece_rows(p)],
-            samples.at[tm, core, piece_rows(p)],
+            rec_ref.at[pl.ds(piece_start(core, p), piece)],
+            samples.at[tm, piece_in_block(core, p)],
             span_sems,
             (p,),
             other_tm,
@@ -211,16 +231,12 @@
     for copy in span_copies:
         copy.start()
     core_copies = [
-        remote(rec_ref, samples.at[tm, core], core_sems, (0,), other_core),
-        remote(trail_ref, samples.at[2, core], core_sems, (1,), other_core),
+        remote(rec_ref, samples.at[tm, half(core)], core_sems, (0,), other_core),
+        remote(trail_ref, samples.at[2, half(core)], core_sems, (1,), other_core),
         remote(filt_ref, filters.at[core], core_sems, (2,), other_core),
     ]
     for copy in core_copies:
         copy.start()
-
-    samples[tm, core] = rec_ref[...]
-    samples[2, core] = trail_ref[...]
-    filters[core] = filt_ref[...]
 
     first_bin = (tm * 2 + core) * width
     unit = 2.0 * math.pi / window
@@ -261,57 +277,59 @@
     def _():
         raw[rim + block_rows : 2 * rim + block_rows] = jnp.zeros((rim, raw.shape[1]), raw.dtype)
 
-    pass_copies = [
-        remote(
-            samples.at[1 - tm, core, piece_rows(p)],
-            samples.at[1 - tm, core, piece_rows(p)],
-            pass_sems,
-            (p,),
-            other_core,
-        )
-        for p in range(PIECES)
-    ]
-    arriving = [
-        remote(
-            rec_ref.at[piece_rows(p)],
-            samples.at[1 - tm, core, piece_rows(p)],
-            span_sems,
-            (p,),
-            other_tm,
-        )
-        for p in range(PIECES)
-    ]
-    for p in range(PIECES):
-        arriving[p].wait_recv()
-        pass_copies[p].start()
-
-    def transform(half):
-        pair = samples[0:2, half].reshape(2 * rows, hop)
-        later = samples[1:3, half].reshape(2 * rows, hop)
-        product = jnp.dot(pair, table[:hop], preferred_element_type=jnp.float32) + jnp.dot(
-            later, table[hop:], preferred_element_type=jnp.float32
-        )
-        product = product.astype(jnp.bfloat16)
-        at = pl.ds(pl.multiple_of(rim + half * rows, rim), rows)
-        raw[at, 0:width] = product[:rows, :width]
-        raw[at, width : 2 * width] = product[rows:, :width]
-        raw[at, 2 * width : 3 * width] = product[:rows, width:]
-        raw[at, 3 * width : 4 * width] = product[rows:, width:]
-
-    transform(core)
-    other = 1 - core
-    remote(rec_ref, samples.at[tm, other], core_sems, (0,), other_core).wait_recv()
-    remote(trail_ref, samples.at[2, other], core_sems, (1,), other_core).wait_recv()
+    for copy in own_copies:
+        copy.wait()
     remote(filt_ref, filters.at[other], core_sems, (2,), other_core).wait_recv()
-    for p in range(PIECES):
-        remote(
-            samples.at[1 - tm, core, piece_rows(p)],
-            samples.at[1 - tm, other, piece_rows(p)],
-            pass_sems,
-            (p,),
-            other_core,
-        ).wait_recv()
-    transform(other)
+    for which in range(2):
+        weights = jnp.transpose(filters[which].astype(jnp.float32))
+        wide = jnp.concatenate([weights, jnp.zeros((rows, 128 - taps), jnp.float32)], axis=1)
+        for p in range(PIECES):
+            rolled = pltpu.roll(
+                wide[p * piece : (p + 1) * piece], 0, 1, stride=1, stride_axis=0
+            )
+            bands[which * PIECES + p] = rolled.astype(jnp.bfloat16)
+
+    remote(rec_ref, samples.at[tm, half(other)], core_sems, (0,), other_core).wait_recv()
+    remote(trail_ref, samples.at[2, half(other)], core_sems, (1,), other_core).wait_recv()
+
+    own_slot = lax.rem(me, window_slots)
+
+    def whiten(tile):
+        near = raw[tile * piece : tile * piece + piece + taps]
+        predicted = jnp.dot(
+            bands[tile][:, : piece + taps], near, preferred_element_type=jnp.float32
+        )
+        mine = raw[rim + tile * piece : rim + (tile + 1) * piece].astype(jnp.float32)
+        gathered[own_slot, tile * piece : (tile + 1) * piece] = (mine - predicted).astype(
+            jnp.bfloat16
+        )
+
+    tiers = [((PIECES - 1) * piece, 2 * piece)]
+    for p in range(1, PIECES):
+        tiers += [((PIECES - 1 - p) * piece, piece), ((PIECES + p) * piece, piece)]
+
+    def block_copy(direction, distance, tier, sem):
+        start, count = tiers[tier]
+        source = me - distance if direction == 0 else me + distance
+        slot = lax.rem(jnp.clip(source, 0, chan_count - 1), window_slots)
+        at = gathered.at[slot, pl.ds(start, count)]
+        return remote(at, at, block_sems, (direction, sem, tier), right if direction == 0 else left)
+
+    def outgoing(direction, distance, tier):
+        return block_copy(direction, distance, tier, distance)
+
+    def landed(direction, distance, tier):
+        return block_copy(direction, distance, tier, distance - 1)
+
+    ahead = (has_right, has_left)
+
+    def send_own(*chosen):
+        for direction in range(2):
+
+            @pl.when(ahead[direction])
+            def _():
+                for tier in chosen:
+                    outgoing(direction, 0, tier).start()
 
     to_right = remote(raw.at[block_rows : block_rows + rim], raw.at[0:rim], rim_sems, (0,), right)
     to_left = remote(
@@ -321,83 +339,53 @@
         (1,),
         left,
     )
-
-    @pl.when(has_right)
-    def _():
-        to_right.start()
-
-    @pl.when(has_left)
-    def _():
-        to_left.start()
-
-    own_slot = lax.rem(me, window_slots)
-
-    def whiten(tile):
-        weights = filters[tile * TILE // rows, tile * TILE % rows : tile * TILE % rows + TILE]
-        wide = jnp.concatenate(
-            [weights.astype(jnp.float32), jnp.zeros((TILE, TILE), jnp.float32)], axis=1
-        )
-        band = pltpu.roll(wide, 0, 1, stride=1, stride_axis=0).astype(jnp.bfloat16)
-        near = raw[tile * TILE : tile * TILE + 2 * TILE]
-        predicted = jnp.dot(band, near, preferred_element_type=jnp.float32)
-        mine = raw[rim + tile * TILE : rim + tile * TILE + TILE].astype(jnp.float32)
-        gathered[own_slot, tile * TILE : tile * TILE + TILE] = (mine - predicted).astype(
-            jnp.bfloat16
-        )
-
-    def block_copy(direction, distance, tier):
-        start, count = TIERS[tier]
-        source = me - distance if direction == 0 else me + distance
-        slot = lax.rem(jnp.clip(source, 0, chan_count - 1), window_slots)
-        at = gathered.at[slot, pl.ds(start, count)]
-        return remote(
-            at, at, block_sems, (direction, distance, tier), right if direction == 0 else left
-        )
-
-    def landed(direction, distance, tier):
-        start, count = TIERS[tier]
-        source = me - distance if direction == 0 else me + distance
-        slot = lax.rem(jnp.clip(source, 0, chan_count - 1), window_slots)
-        at = gathered.at[slot, pl.ds(start, count)]
-        return remote(
-            at, at, block_sems, (direction, distance - 1, tier), right if direction == 0 else left
-        )
-
-    ahead = (has_right, has_left)
-
-    def send_own(tier):
-        for direction in range(2):
-
-            @pl.when(ahead[direction])
+    pass_copies = []
+    for p in range(PIECES):
+        mine = samples.at[1 - tm, piece_in_block(core, p)]
+        theirs = samples.at[1 - tm, piece_in_block(other, p)]
+        remote(mine, mine, span_sems, (p,), other_tm).wait_recv()
+        passing = remote(mine, mine, pass_sems, (p,), other_core)
+        passing.start()
+        pass_copies.append(passing)
+        remote(theirs, theirs, pass_sems, (p,), other_core).wait_recv()
+
+        low, high = (PIECES - 1 - p) * piece, (PIECES + p) * piece
+        first = [samples[0:2, at : at + piece].reshape(2 * piece, hop) for at in (low, high)]
+        second = [samples[1:3, at : at + piece].reshape(2 * piece, hop) for at in (low, high)]
+        product = jnp.dot(
+            jnp.concatenate(first, axis=0), table[:hop], preferred_element_type=jnp.float32
+        ) + jnp.dot(
+            jnp.concatenate(second, axis=0), table[hop:], preferred_element_type=jnp.float32
+        )
+        product = product.astype(jnp.bfloat16)
+        for index, at in enumerate((low, high)):
+            for segment in range(2):
+                found = product[(2 * index + segment) * piece : (2 * index + segment + 1) * piece]
+                where = pl.ds(rim + at, piece)
+                raw[where, segment * width : (segment + 1) * width] = found[:, :width]
+                raw[where, (2 + segment) * width : (3 + segment) * width] = found[:, width:]
+        if p == PIECES - 1:
+
+            @pl.when(has_right)
             def _():
-                block_copy(direction, 0, tier).start()
-
-    whiten(1)
-    whiten(2)
-    send_own(0)
-
-    @pl.when(has_left)
-    def _():
-        remote(raw.at[0:rim], raw.at[0:rim], rim_sems, (0,), right).wait_recv()
-
-    whiten(0)
-    send_own(1)
-
-    @pl.when(has_right)
-    def _():
-        at = raw.at[rim + block_rows : 2 * rim + block_rows]
-        remote(at, at, rim_sems, (1,), left).wait_recv()
-
-    whiten(3)
-    send_own(2)
+                to_right.start()
+
+            @pl.when(has_left)
+            def _():
+                to_left.start()
+
+        if p > 0:
+            whiten(PIECES - p)
+            whiten(PIECES + p - 1)
+            send_own(*((0,) if p == 1 else (2 * p - 3, 2 * p - 2)))
 
     furthest = min(REACH, chan_count - 1)
 
     def exists(direction, distance):
         return me - distance >= 0 if direction == 0 else me + distance < chan_count
 
-    for distance in range(1, furthest + 1):
-        for tier in range(len(TIERS)):
+    def advance(distance, chosen):
+        for tier in chosen:
             for direction in range(2):
 
                 @pl.when(exists(direction, distance))
@@ -408,48 +396,86 @@
 
                     @pl.when(jnp.logical_and(exists(direction, distance), ahead[direction]))
                     def _():
-                        block_copy(direction, distance, tier).start()
+                        outgoing(direction, distance, tier).start()
+
+    early = 3
+    advance(1, range(early))
+
+    @pl.when(has_left)
+    def _():
+        remote(raw.at[0:rim], raw.at[0:rim], rim_sems, (0,), right).wait_recv()
+
+    whiten(0)
+    send_own(2 * PIECES - 3)
+
+    @pl.when(has_right)
+    def _():
+        at = raw.at[rim + block_rows : 2 * rim + block_rows]
+        remote(at, at, rim_sems, (1,), left).wait_recv()
+
+    whiten(2 * PIECES - 1)
+    send_own(2 * PIECES - 2)
+
+    @pl.when(has_right)
+    def _():
+        to_right.wait_send()
+
+    @pl.when(has_left)
+    def _():
+        to_left.wait_send()
+
+    own = gathered[own_slot]
+    middle = own.shape[1] // 2
+    raw[0:block_rows] = jnp.concatenate([own[:, middle:], -own[:, :middle]], axis=1)
+    contract = (((1,), (1,)), ((), ()))
+
+    def cross(slot):
+        partner = gathered[slot]
+        for part, side in enumerate((gathered[own_slot], raw[0:block_rows])):
+            crossed[slot, part] = (
+                lax.dot_general(side, partner, contract, preferred_element_type=jnp.float32)
+                * scaling
+            )
+
+    cross(own_slot)
+
+    for distance in range(1, furthest + 1):
+        advance(distance, range(early if distance == 1 else 0, len(tiers)))
+        for direction in range(2):
+
+            @pl.when(exists(direction, distance))
+            def _():
+                source = me - distance if direction == 0 else me + distance
+                cross(lax.rem(jnp.clip(source, 0, chan_count - 1), window_slots))
 
     for copy in span_copies + core_copies + pass_copies:
         copy.wait_send()
 
-    @pl.when(has_right)
-    def _():
-        to_right.wait_send()
-
-    @pl.when(has_left)
-    def _():
-        to_left.wait_send()
-
     for distance in range(furthest):
-        for tier in range(len(TIERS)):
+        for tier in range(len(tiers)):
             for direction in range(2):
 
                 @pl.when(jnp.logical_and(exists(direction, distance), ahead[direction]))
                 def _():
-                    block_copy(direction, distance, tier).wait_send()
-
-
-def cross_kernel(window_slots, scaling, pairs_ref, gathered, out_ref):
-    slot = pl.program_id(0)
-    me = lax.rem(lax.axis_index("chan"), window_slots)
-    partner = pairs_ref[0, slot]
-    half = gathered.shape[2] // 2
-    contract = (((1,), (1,)), ((), ()))
-
-    @pl.when(partner >= 0)
-    def _():
-        own = gathered[me]
-        right_side = gathered[lax.rem(jnp.maximum(partner, 0), window_slots)]
-        turned = jnp.concatenate([own[:, half:], -own[:, :half]], axis=1)
-        real = lax.dot_general(own, right_side, contract, preferred_element_type=jnp.float32)
-        out_ref[0, 0, 0, 0] = real * scaling
-        imag = lax.dot_general(turned, right_side, contract, preferred_element_type=jnp.float32)
-        out_ref[0, 0, 0, 1] = imag * scaling
-
-    @pl.when(partner < 0)
-    def _():
-        out_ref[...] = jnp.zeros_like(out_ref)
+                    outgoing(direction, distance, tier).wait_send()
+
+
+def slot_kernel(window_slots, pairs_ref, crossed, out_ref, blank, sems):
+    blank[...] = jnp.zeros_like(blank)
+    for slot in range(SLOTS):
+        partner = pairs_ref[0, slot]
+        source = crossed.at[lax.rem(jnp.maximum(partner, 0), window_slots)]
+
+        @pl.when(partner >= 0)
+        def _():
+            pltpu.make_async_copy(source, out_ref.at[0, slot, 0], sems.at[slot]).start()
+
+        @pl.when(partner < 0)
+        def _():
+            pltpu.make_async_copy(blank, out_ref.at[0, slot, 0], sems.at[slot]).start()
+
+    for slot in range(SLOTS):
+        pltpu.make_async_copy(blank, out_ref.at[0, slot, 0], sems.at[slot]).wait()
 
 
 def fused(recording, trailing, whiten_filter, pair_list):
@@ -462,37 +488,43 @@
     depth = 2 * width
     furthest = min(REACH, chan_count - 1)
     vmem = pl.BlockSpec(memory_space=pltpu.VMEM)
-    gathered = pl.pallas_call(
-        functools.partial(spectra_kernel, chan_count, window_slots),
-        out_shape=jax.ShapeDtypeStruct((window_slots, block_rows, 2 * depth), jnp.bfloat16),
-        in_specs=[vmem] * 3,
+    anywhere = pl.BlockSpec(memory_space=pl.ANY)
+    tier_count = 2 * PIECES - 1
+    crossed = pl.pallas_call(
+        functools.partial(spectra_kernel, chan_count, window_slots, 1.0 / math.sqrt(depth)),
+        out_shape=jax.ShapeDtypeStruct((window_slots, 2, block_rows, block_rows), jnp.float32),
+        in_specs=[pl.BlockSpec(memory_space=pltpu.HBM)] * 3,
         out_specs=vmem,
         scratch_shapes=[
-            pltpu.VMEM((3, 2, rows, hop), jnp.bfloat16),
-            pltpu.VMEM((2, rows, taps), jnp.bfloat16),
+            pltpu.VMEM((3, block_rows, hop), jnp.bfloat16),
+            pltpu.VMEM((2, taps, rows), jnp.bfloat16),
+            pltpu.VMEM((2 * PIECES, rows // PIECES, 128), jnp.bfloat16),
             pltpu.VMEM((2 * hop, 2 * width), jnp.bfloat16),
             pltpu.VMEM((4, 2 * hop // STEP, width), jnp.float32),
             pltpu.VMEM((block_rows + taps, 2 * depth), jnp.bfloat16),
+            pltpu.VMEM((window_slots, block_rows, 2 * depth), jnp.bfloat16),
+            pltpu.SemaphoreType.DMA((3,)),
             pltpu.SemaphoreType.DMA((2, PIECES)),
             pltpu.SemaphoreType.DMA((2, 3)),
             pltpu.SemaphoreType.DMA((2, PIECES)),
             pltpu.SemaphoreType.DMA((2, 2)),
-            pltpu.SemaphoreType.DMA((2, 2, furthest, len(TIERS))),
+            pltpu.SemaphoreType.DMA((2, 2, furthest, tier_count)),
         ],
-        compiler_params=pltpu.CompilerParams(collective_id=0, has_side_effects=True),
-    )(recording, trailing, whiten_filter)
+        compiler_params=pltpu.CompilerParams(
+            collective_id=0, has_side_effects=True, vmem_limit_bytes=16 * 2**20
+        ),
+    )(recording, trailing, whiten_filter.T)
     return pl.pallas_call(
-        functools.partial(cross_kernel, window_slots, 1.0 / math.sqrt(depth)),
+        functools.partial(slot_kernel, window_slots),
         out_shape=jax.ShapeDtypeStruct((1, SLOTS, 1, 2, block_rows, block_rows), jnp.float32),
-        grid_spec=pltpu.PrefetchScalarGridSpec(
-            num_scalar_prefetch=1,
-            grid=(SLOTS,),
-            in_specs=[vmem],
-            out_specs=pl.BlockSpec(
-                (1, 1, 1, 2, block_rows, block_rows), lambda slot, pairs: (0, slot, 0, 0, 0, 0)
-            ),
-        ),
-    )(pair_list, gathered)
+        in_specs=[pl.BlockSpec(memory_space=pltpu.SMEM), anywhere],
+        out_specs=anywhere,
+        scratch_shapes=[
+            pltpu.VMEM((2, block_rows, block_rows), jnp.float32),
+            pltpu.SemaphoreType.DMA((SLOTS,)),
+        ],
+        compiler_params=pltpu.CompilerParams(vmem_limit_bytes=8 * 2**20),
+    )(pair_list, crossed)
 
 
 def local(recording, trailing, whiten_filter, pair_list):

time: 41.1 us -> 37.8 us (0.920)
  Pallas kernels: 39.7 us -> 34.9 us
  local copies, waits for them, and re-layouts: 1.43 us -> 2.63 us
    pallas_call x1, Pallas kernels: 4.56 us -> 1.89 us  [fused(): pl.pallas_call(functools.partial(slot_kernel, window_slots), out_shape=ja...]
    pallas_call x1, Pallas kernels: 35.1 us -> 33 us  [fused(): pl.pallas_call(functools.partial(spectra_kernel, chan_count, window_slots...]
    unnamed x1 -> x8, local copies, waits for them, and re-layouts: 1.43 us -> 2.63 us
where the time goes in v2:
time: 37.8 us; the launch traced here: 37.5 us
  Pallas kernels  34.9 us (92%)
  local copies, waits for them, and re-layouts  2.63 us (7%)
    pallas_call x1, Pallas kernels, fused(): pl.pallas_call(functools.partial(spectra_kernel, chan_count, window_slots...  33 us
    unnamed x8, local copies, waits for them, and re-layouts  2.63 us
    pallas_call x1, Pallas kernels, fused(): pl.pallas_call(functools.partial(slot_kernel, window_slots), out_shape=ja...  1.89 us

profile of v2, /device:TPU:0, one launch (start us, length us, event | category | flops | bytes accessed | tf_op | source)
XLA Modules:
  0.0 37.5 jit_solution(14593534559606290098)
XLA Ops:
  0.0 0.0 copy-start.3
  0.0 0.0 copy-start
  0.0 1.0 %copy-done = bf16[128,1024]{1,0:T(8,128)(2,1)S(1)} copy-done((bf16[128,1024]{1,0:T(8,128)(2,1)S(1)}, bf16[128,1024]{1,0:T(8,128)(2,1)}, u32[]{:S(2)}) %copy-start) | copy-done | bytes 262168
  1.0 0.0 copy-start.1
  1.0 0.9 %copy-done.1 = bf16[128,1024]{1,0:T(8,128)(2,1)S(1)} copy-done((bf16[128,1024]{1,0:T(8,128)(2,1)S(1)}, bf16[128,1024]{1,0:T(8,128)(2,1)}, u32[]{:S(2)}) %copy-start.1) | copy-done | bytes 262168
  1.9 0.0 copy-start.2
  1.9 0.7 %copy-done.2 = bf16[128,64]{0,1:T(8,128)(2,1)S(1)} copy-done((bf16[128,64]{0,1:T(8,128)(2,1)S(1)}, bf16[128,64]{0,1:T(8,128)(2,1)}, u32[]{:S(2)}) %copy-start.2) | copy-done | bytes 16408
  2.6 33.0 %shard_map.46.crossed = f32[4,2,256,256]{3,2,1,0:T(8,128)S(1)} custom-call(bf16[128,1024]{1,0:T(8,128)(2,1)S(1)} %copy-done, bf16[128,1024]{1,0:T(8,128)(2,1)S(1)} %copy-done.1, bf16[64,128]{1,0:T(8,128)(2,1)S(1)} %bitcast.1), custom_call_target="tpu_custom_call" | custom-call | tf_op jit(solution)/shard_map/pallas_call | solution.py:493
  35.6 0.0 copy-done.3
  35.6 1.9 %shard_map.47 = f32[1,4,1,2,256,256]{5,4,3,2,1,0:T(8,128)} custom-call(s32[1,4]{1,0:T(1,128)S(1)} %copy-done.3, f32[4,2,256,256]{3,2,1,0:T(8,128)S(1)} %shard_map.46.crossed), custom_call_target="tpu_custom_call" | custom-call | tf_op jit(solution)/shard_map/pallas_call | solution.py:517
Async XLA Ops:
  0.0 35.6 %copy-start.3 = (s32[1,4]{1,0:T(1,128)S(1)}, s32[1,4]{1,0:T(1,128)}, u32[]{:S(2)}) copy-start(s32[1,4]{1,0:T(1,128)} %pairs_ref.1) | copy-start | bytes 52
  0.0 1.0 %copy-start = (bf16[128,1024]{1,0:T(8,128)(2,1)S(1)}, bf16[128,1024]{1,0:T(8,128)(2,1)}, u32[]{:S(2)}) copy-start(bf16[128,1024]{1,0:T(8,128)(2,1)} %rec_ref.1) | copy-start | bytes 786436
  1.0 0.9 %copy-start.1 = (bf16[128,1024]{1,0:T(8,128)(2,1)S(1)}, bf16[128,1024]{1,0:T(8,128)(2,1)}, u32[]{:S(2)}) copy-start(bf16[128,1024]{1,0:T(8,128)(2,1)} %trail_ref.1) | copy-start | bytes 786436
  1.9 0.7 %copy-start.2 = (bf16[128,64]{0,1:T(8,128)(2,1)S(1)}, bf16[128,64]{0,1:T(8,128)(2,1)}, u32[]{:S(2)}) copy-start(bf16[128,64]{0,1:T(8,128)(2,1)} %param.6) | copy-start | bytes 49156

commit v3 on v2

--- a/solution.py
+++ b/solution.py
@@ -136,7 +136,6 @@
 
 def spectra_kernel(
     chan_count,
-    window_slots,
     scaling,
     rec_ref,
     trail_ref,
@@ -149,12 +148,15 @@
     coarse,
     raw,
     gathered,
+    turned,
+    products,
     local_sems,
     span_sems,
     core_sems,
     pass_sems,
-    rim_sems,
+    filter_sems,
     block_sems,
+    out_sems,
 ):
     me = lax.axis_index("chan")
     tm = lax.axis_index("tm")
@@ -191,27 +193,23 @@
     pl.semaphore_signal(barrier, inc=1, device_id=other_tm, device_id_type=MESH)
     pl.semaphore_signal(barrier, inc=1, device_id=other_core, device_id_type=MESH)
 
-    @pl.when(has_left)
-    def _():
-        pl.semaphore_signal(barrier, inc=1, device_id=left, device_id_type=MESH)
-
-    @pl.when(has_right)
-    def _():
-        pl.semaphore_signal(barrier, inc=1, device_id=right, device_id_type=MESH)
+    for distance in range(1, chan_count):
+        peer = {"chan": lax.rem(me + distance, chan_count)}
+        pl.semaphore_signal(barrier, inc=1, device_id=peer, device_id_type=MESH)
 
     own_copies = [
         pltpu.make_async_copy(rec_ref, samples.at[tm, half(core)], local_sems.at[0]),
         pltpu.make_async_copy(trail_ref, samples.at[2, half(core)], local_sems.at[1]),
-        pltpu.make_async_copy(filt_ref, filters.at[core], local_sems.at[2]),
+        pltpu.make_async_copy(filt_ref, filters.at[core, me], local_sems.at[2]),
     ]
     for copy in own_copies:
         copy.start()
 
-    pl.semaphore_wait(barrier, 2 + has_left.astype(jnp.int32) + has_right.astype(jnp.int32))
+    pl.semaphore_wait(barrier, 1 + chan_count)
 
     def piece_start(which, step):
         return pl.multiple_of(
-            (1 - which) * (PIECES - 1 - step) * piece + which * step * piece, piece
+            (1 - which) * step * piece + which * (PIECES - 1 - step) * piece, piece
         )
 
     def piece_in_block(which, step):
@@ -233,10 +231,25 @@
     core_copies = [
         remote(rec_ref, samples.at[tm, half(core)], core_sems, (0,), other_core),
         remote(trail_ref, samples.at[2, half(core)], core_sems, (1,), other_core),
-        remote(filt_ref, filters.at[core], core_sems, (2,), other_core),
     ]
     for copy in core_copies:
         copy.start()
+
+    def exists(direction, distance):
+        return me - distance >= 0 if direction == 0 else me + distance < chan_count
+
+    def weights_copy(direction, distance):
+        device = {"chan": me + distance if direction == 0 else me - distance}
+        return remote(
+            filt_ref, filters.at[core, me], filter_sems, (direction, distance - 1), device
+        )
+
+    for distance in range(1, chan_count):
+        for direction in range(2):
+
+            @pl.when(exists(1 - direction, distance))
+            def _():
+                weights_copy(direction, distance).start()
 
     first_bin = (tm * 2 + core) * width
     unit = 2.0 * math.pi / window
@@ -269,50 +282,26 @@
 
     lax.fori_loop(0, parts, fill, 0)
 
-    @pl.when(jnp.logical_not(has_left))
-    def _():
-        raw[0:rim] = jnp.zeros((rim, raw.shape[1]), raw.dtype)
-
-    @pl.when(jnp.logical_not(has_right))
-    def _():
-        raw[rim + block_rows : 2 * rim + block_rows] = jnp.zeros((rim, raw.shape[1]), raw.dtype)
+    edge = jnp.zeros((rim, raw.shape[1]), raw.dtype)
+    raw[0:rim] = edge
+    raw[rim + chan_count * block_rows :] = edge
 
     for copy in own_copies:
         copy.wait()
-    remote(filt_ref, filters.at[other], core_sems, (2,), other_core).wait_recv()
-    for which in range(2):
-        weights = jnp.transpose(filters[which].astype(jnp.float32))
-        wide = jnp.concatenate([weights, jnp.zeros((rows, 128 - taps), jnp.float32)], axis=1)
-        for p in range(PIECES):
-            rolled = pltpu.roll(
-                wide[p * piece : (p + 1) * piece], 0, 1, stride=1, stride_axis=0
-            )
-            bands[which * PIECES + p] = rolled.astype(jnp.bfloat16)
-
     remote(rec_ref, samples.at[tm, half(other)], core_sems, (0,), other_core).wait_recv()
     remote(trail_ref, samples.at[2, half(other)], core_sems, (1,), other_core).wait_recv()
 
-    own_slot = lax.rem(me, window_slots)
-
-    def whiten(tile):
-        near = raw[tile * piece : tile * piece + piece + taps]
-        predicted = jnp.dot(
-            bands[tile][:, : piece + taps], near, preferred_element_type=jnp.float32
-        )
-        mine = raw[rim + tile * piece : rim + (tile + 1) * piece].astype(jnp.float32)
-        gathered[own_slot, tile * piece : (tile + 1) * piece] = (mine - predicted).astype(
-            jnp.bfloat16
-        )
-
-    tiers = [((PIECES - 1) * piece, 2 * piece)]
-    for p in range(1, PIECES):
-        tiers += [((PIECES - 1 - p) * piece, piece), ((PIECES + p) * piece, piece)]
+    def own_rows(block, start, count):
+        return pl.ds(pl.multiple_of(rim + block * block_rows + start, piece), count)
+
+    tiers = [(which, p) for which in range(2) for p in range(PIECES)]
 
     def block_copy(direction, distance, tier, sem):
-        start, count = tiers[tier]
+        which, p = tiers[tier]
+        here = core if which == 0 else other
         source = me - distance if direction == 0 else me + distance
-        slot = lax.rem(jnp.clip(source, 0, chan_count - 1), window_slots)
-        at = gathered.at[slot, pl.ds(start, count)]
+        source = jnp.clip(source, 0, chan_count - 1)
+        at = raw.at[own_rows(source, here * rows + piece_start(here, p), piece)]
         return remote(at, at, block_sems, (direction, sem, tier), right if direction == 0 else left)
 
     def outgoing(direction, distance, tier):
@@ -323,69 +312,116 @@
 
     ahead = (has_right, has_left)
 
-    def send_own(*chosen):
+    def transform(which, p, tier):
+        at = which * rows + piece_start(which, p)
+        chosen = pl.ds(pl.multiple_of(at, piece), piece)
+        product = jnp.dot(
+            samples[0:2, chosen].reshape(2 * piece, hop),
+            table[:hop],
+            preferred_element_type=jnp.float32,
+        ) + jnp.dot(
+            samples[1:3, chosen].reshape(2 * piece, hop),
+            table[hop:],
+            preferred_element_type=jnp.float32,
+        )
+        product = product.astype(jnp.bfloat16)
+        where = own_rows(me, at, piece)
+        for segment in range(2):
+            found = product[segment * piece : (segment + 1) * piece]
+            raw[where, segment * width : (segment + 1) * width] = found[:, :width]
+            raw[where, (2 + segment) * width : (3 + segment) * width] = found[:, width:]
         for direction in range(2):
 
             @pl.when(ahead[direction])
             def _():
-                for tier in chosen:
-                    outgoing(direction, 0, tier).start()
-
-    to_right = remote(raw.at[block_rows : block_rows + rim], raw.at[0:rim], rim_sems, (0,), right)
-    to_left = remote(
-        raw.at[rim : 2 * rim],
-        raw.at[rim + block_rows : 2 * rim + block_rows],
-        rim_sems,
-        (1,),
-        left,
-    )
+                outgoing(direction, 0, tier).start()
+
     pass_copies = []
     for p in range(PIECES):
         mine = samples.at[1 - tm, piece_in_block(core, p)]
-        theirs = samples.at[1 - tm, piece_in_block(other, p)]
         remote(mine, mine, span_sems, (p,), other_tm).wait_recv()
         passing = remote(mine, mine, pass_sems, (p,), other_core)
         passing.start()
         pass_copies.append(passing)
+        transform(core, p, p)
+
+    for distance in range(1, chan_count):
+        for direction in range(2):
+
+            @pl.when(exists(direction, distance))
+            def _():
+                at = filters.at[core, me - distance if direction == 0 else me + distance]
+                remote(at, at, filter_sems, (direction, distance - 1), other_core).wait_recv()
+
+    core_copies.append(
+        remote(filters.at[core], filters.at[core], core_sems, (2,), other_core)
+    )
+    core_copies[-1].start()
+
+    for p in range(PIECES):
+        theirs = samples.at[1 - tm, piece_in_block(other, p)]
         remote(theirs, theirs, pass_sems, (p,), other_core).wait_recv()
-
-        low, high = (PIECES - 1 - p) * piece, (PIECES + p) * piece
-        first = [samples[0:2, at : at + piece].reshape(2 * piece, hop) for at in (low, high)]
-        second = [samples[1:3, at : at + piece].reshape(2 * piece, hop) for at in (low, high)]
-        product = jnp.dot(
-            jnp.concatenate(first, axis=0), table[:hop], preferred_element_type=jnp.float32
-        ) + jnp.dot(
-            jnp.concatenate(second, axis=0), table[hop:], preferred_element_type=jnp.float32
-        )
-        product = product.astype(jnp.bfloat16)
-        for index, at in enumerate((low, high)):
-            for segment in range(2):
-                found = product[(2 * index + segment) * piece : (2 * index + segment + 1) * piece]
-                where = pl.ds(rim + at, piece)
-                raw[where, segment * width : (segment + 1) * width] = found[:, :width]
-                raw[where, (2 + segment) * width : (3 + segment) * width] = found[:, width:]
-        if p == PIECES - 1:
-
-            @pl.when(has_right)
-            def _():
-                to_right.start()
-
-            @pl.when(has_left)
-            def _():
-                to_left.start()
-
-        if p > 0:
-            whiten(PIECES - p)
-            whiten(PIECES + p - 1)
-            send_own(*((0,) if p == 1 else (2 * p - 3, 2 * p - 2)))
-
-    furthest = min(REACH, chan_count - 1)
-
-    def exists(direction, distance):
-        return me - distance >= 0 if direction == 0 else me + distance < chan_count
-
-    def advance(distance, chosen):
-        for tier in chosen:
+        transform(other, p, PIECES + p)
+
+    remote(filters.at[other], filters.at[other], core_sems, (2,), other_core).wait_recv()
+
+    def spread(block, carry):
+        for which in range(2):
+            weights = jnp.transpose(filters[which, block].astype(jnp.float32))
+            wide = jnp.concatenate([weights, jnp.zeros((rows, 128 - taps), jnp.float32)], axis=1)
+            for p in range(PIECES):
+                rolled = pltpu.roll(
+                    wide[p * piece : (p + 1) * piece], 0, 1, stride=1, stride_axis=0
+                )
+                bands[block, which * PIECES + p] = rolled.astype(jnp.bfloat16)
+        return carry
+
+    lax.fori_loop(0, chan_count, spread, 0)
+
+    def whiten(block, tile):
+        start = pl.multiple_of(block * block_rows + tile * piece, piece)
+        near = raw[pl.ds(start, piece + taps)]
+        predicted = jnp.dot(
+            bands[block, tile][:, : piece + taps], near, preferred_element_type=jnp.float32
+        )
+        mine = near[rim : rim + piece].astype(jnp.float32)
+        gathered[block, tile * piece : (tile + 1) * piece] = (mine - predicted).astype(
+            jnp.bfloat16
+        )
+
+    contract = (((1,), (1,)), ((), ()))
+
+    def cross(block, index):
+        partner = gathered[block]
+        for part, side in enumerate((gathered[me], turned[...])):
+            products[block, part] = (
+                lax.dot_general(side, partner, contract, preferred_element_type=jnp.float32)
+                * scaling
+            )
+        pltpu.make_async_copy(products.at[block], crossed.at[block], out_sems.at[index]).start()
+
+    tile_count = 2 * PIECES
+    for tile in range(1, tile_count - 1):
+        whiten(me, tile)
+
+    def finish_own():
+        whiten(me, 0)
+        whiten(me, tile_count - 1)
+        own = gathered[me]
+        middle = own.shape[1] // 2
+        turned[...] = jnp.concatenate([own[:, middle:], -own[:, :middle]], axis=1)
+        cross(me, 0)
+
+    def finish(direction, distance):
+        @pl.when(exists(direction, distance))
+        def _():
+            block = me - distance if direction == 0 else me + distance
+            whiten(block, 0 if direction == 0 else tile_count - 1)
+            cross(block, 2 * distance - 1 + direction)
+
+    furthest = chan_count - 1
+    for distance in range(1, chan_count):
+        for tier in range(len(tiers)):
             for direction in range(2):
 
                 @pl.when(exists(direction, distance))
@@ -398,58 +434,33 @@
                     def _():
                         outgoing(direction, distance, tier).start()
 
-    early = 3
-    advance(1, range(early))
-
-    @pl.when(has_left)
-    def _():
-        remote(raw.at[0:rim], raw.at[0:rim], rim_sems, (0,), right).wait_recv()
-
-    whiten(0)
-    send_own(2 * PIECES - 3)
-
-    @pl.when(has_right)
-    def _():
-        at = raw.at[rim + block_rows : 2 * rim + block_rows]
-        remote(at, at, rim_sems, (1,), left).wait_recv()
-
-    whiten(2 * PIECES - 1)
-    send_own(2 * PIECES - 2)
-
-    @pl.when(has_right)
-    def _():
-        to_right.wait_send()
-
-    @pl.when(has_left)
-    def _():
-        to_left.wait_send()
-
-    own = gathered[own_slot]
-    middle = own.shape[1] // 2
-    raw[0:block_rows] = jnp.concatenate([own[:, middle:], -own[:, :middle]], axis=1)
-    contract = (((1,), (1,)), ((), ()))
-
-    def cross(slot):
-        partner = gathered[slot]
-        for part, side in enumerate((gathered[own_slot], raw[0:block_rows])):
-            crossed[slot, part] = (
-                lax.dot_general(side, partner, contract, preferred_element_type=jnp.float32)
-                * scaling
-            )
-
-    cross(own_slot)
-
-    for distance in range(1, furthest + 1):
-        advance(distance, range(early if distance == 1 else 0, len(tiers)))
+            if tier == PIECES:
+                if distance == 1:
+                    finish_own()
+                else:
+                    for direction in range(2):
+                        finish(direction, distance - 1)
+
         for direction in range(2):
 
             @pl.when(exists(direction, distance))
             def _():
-                source = me - distance if direction == 0 else me + distance
-                cross(lax.rem(jnp.clip(source, 0, chan_count - 1), window_slots))
+                block = me - distance if direction == 0 else me + distance
+                for tile in range(tile_count - 1):
+                    whiten(block, tile + 1 if direction == 0 else tile)
+
+    for direction in range(2):
+        finish(direction, furthest)
 
     for copy in span_copies + core_copies + pass_copies:
         copy.wait_send()
+
+    for distance in range(1, chan_count):
+        for direction in range(2):
+
+            @pl.when(exists(1 - direction, distance))
+            def _():
+                weights_copy(direction, distance).wait_send()
 
     for distance in range(furthest):
         for tier in range(len(tiers)):
@@ -459,78 +470,100 @@
                 def _():
                     outgoing(direction, distance, tier).wait_send()
 
-
-def slot_kernel(window_slots, pairs_ref, crossed, out_ref, blank, sems):
-    blank[...] = jnp.zeros_like(blank)
+    pltpu.make_async_copy(products.at[me], crossed.at[me], out_sems.at[0]).wait()
+    for distance in range(1, chan_count):
+        for direction in range(2):
+
+            @pl.when(exists(direction, distance))
+            def _():
+                block = me - distance if direction == 0 else me + distance
+                index = 2 * distance - 1 + direction
+                pltpu.make_async_copy(
+                    products.at[block], crossed.at[block], out_sems.at[index]
+                ).wait()
+
+
+def slot_kernel(pairs_ref, crossed, out_ref, held, in_sems, out_sems):
+    def fetch(slot):
+        partner = jnp.maximum(pairs_ref[0, slot], 0)
+        return pltpu.make_async_copy(crossed.at[partner], held.at[slot], in_sems.at[slot])
+
+    def store(slot):
+        return pltpu.make_async_copy(held.at[slot], out_ref.at[0, slot, 0], out_sems.at[slot])
+
     for slot in range(SLOTS):
-        partner = pairs_ref[0, slot]
-        source = crossed.at[lax.rem(jnp.maximum(partner, 0), window_slots)]
-
-        @pl.when(partner >= 0)
+
+        @pl.when(pairs_ref[0, slot] >= 0)
         def _():
-            pltpu.make_async_copy(source, out_ref.at[0, slot, 0], sems.at[slot]).start()
-
-        @pl.when(partner < 0)
+            fetch(slot).start()
+
+    for slot in range(SLOTS):
+
+        @pl.when(pairs_ref[0, slot] >= 0)
         def _():
-            pltpu.make_async_copy(blank, out_ref.at[0, slot, 0], sems.at[slot]).start()
+            fetch(slot).wait()
+
+        @pl.when(pairs_ref[0, slot] < 0)
+        def _():
+            held[slot] = jnp.zeros(held.shape[1:], held.dtype)
+
+        store(slot).start()
 
     for slot in range(SLOTS):
-        pltpu.make_async_copy(blank, out_ref.at[0, slot, 0], sems.at[slot]).wait()
+        store(slot).wait()
 
 
 def fused(recording, trailing, whiten_filter, pair_list):
     rows, hop = recording.shape
     chan_count = lax.axis_size("chan")
-    window_slots = min(chan_count, 2 * REACH + 1)
     taps = whiten_filter.shape[1]
     width = FB // (lax.axis_size("tm") * lax.axis_size("freq"))
     block_rows = 2 * rows
     depth = 2 * width
-    furthest = min(REACH, chan_count - 1)
-    vmem = pl.BlockSpec(memory_space=pltpu.VMEM)
     anywhere = pl.BlockSpec(memory_space=pl.ANY)
-    tier_count = 2 * PIECES - 1
     crossed = pl.pallas_call(
-        functools.partial(spectra_kernel, chan_count, window_slots, 1.0 / math.sqrt(depth)),
-        out_shape=jax.ShapeDtypeStruct((window_slots, 2, block_rows, block_rows), jnp.float32),
-        in_specs=[pl.BlockSpec(memory_space=pltpu.HBM)] * 3,
-        out_specs=vmem,
+        functools.partial(spectra_kernel, chan_count, 1.0 / math.sqrt(depth)),
+        out_shape=jax.ShapeDtypeStruct((chan_count, 2, block_rows, block_rows), jnp.float32),
+        in_specs=[anywhere] * 3,
+        out_specs=anywhere,
         scratch_shapes=[
             pltpu.VMEM((3, block_rows, hop), jnp.bfloat16),
-            pltpu.VMEM((2, taps, rows), jnp.bfloat16),
-            pltpu.VMEM((2 * PIECES, rows // PIECES, 128), jnp.bfloat16),
+            pltpu.VMEM((2, chan_count, taps, rows), jnp.bfloat16),
+            pltpu.VMEM((chan_count, 2 * PIECES, rows // PIECES, 128), jnp.bfloat16),
             pltpu.VMEM((2 * hop, 2 * width), jnp.bfloat16),
             pltpu.VMEM((4, 2 * hop // STEP, width), jnp.float32),
-            pltpu.VMEM((block_rows + taps, 2 * depth), jnp.bfloat16),
-            pltpu.VMEM((window_slots, block_rows, 2 * depth), jnp.bfloat16),
+            pltpu.VMEM((chan_count * block_rows + taps, 2 * depth), jnp.bfloat16),
+            pltpu.VMEM((chan_count, block_rows, 2 * depth), jnp.bfloat16),
+            pltpu.VMEM((block_rows, 2 * depth), jnp.bfloat16),
+            pltpu.VMEM((chan_count, 2, block_rows, block_rows), jnp.float32),
             pltpu.SemaphoreType.DMA((3,)),
             pltpu.SemaphoreType.DMA((2, PIECES)),
             pltpu.SemaphoreType.DMA((2, 3)),
             pltpu.SemaphoreType.DMA((2, PIECES)),
-            pltpu.SemaphoreType.DMA((2, 2)),
-            pltpu.SemaphoreType.DMA((2, 2, furthest, tier_count)),
+            pltpu.SemaphoreType.DMA((2, 2, chan_count - 1)),
+            pltpu.SemaphoreType.DMA((2, 2, chan_count - 1, 2 * PIECES)),
+            pltpu.SemaphoreType.DMA((2 * chan_count,)),
         ],
-        compiler_params=pltpu.CompilerParams(
-            collective_id=0, has_side_effects=True, vmem_limit_bytes=16 * 2**20
-        ),
+        compiler_params=pltpu.CompilerParams(collective_id=0, has_side_effects=True),
     )(recording, trailing, whiten_filter.T)
     return pl.pallas_call(
-        functools.partial(slot_kernel, window_slots),
+        slot_kernel,
         out_shape=jax.ShapeDtypeStruct((1, SLOTS, 1, 2, block_rows, block_rows), jnp.float32),
         in_specs=[pl.BlockSpec(memory_space=pltpu.SMEM), anywhere],
         out_specs=anywhere,
         scratch_shapes=[
-            pltpu.VMEM((2, block_rows, block_rows), jnp.float32),
+            pltpu.VMEM((SLOTS, 2, block_rows, block_rows), jnp.float32),
+            pltpu.SemaphoreType.DMA((SLOTS,)),
             pltpu.SemaphoreType.DMA((SLOTS,)),
         ],
-        compiler_params=pltpu.CompilerParams(vmem_limit_bytes=8 * 2**20),
     )(pair_list, crossed)
 
 
 def local(recording, trailing, whiten_filter, pair_list):
     shapes = (recording.shape, trailing.shape, whiten_filter.shape)
     counts = (lax.axis_size("tm"), lax.axis_size("freq"))
-    if shapes == ((128, 1024), (128, 1024), (128, 64)) and counts == (2, 2):
+    whole_reach = 1 < lax.axis_size("chan") <= REACH + 1
+    if shapes == ((128, 1024), (128, 1024), (128, 64)) and counts == (2, 2) and whole_reach:
         return fused(recording, trailing, whiten_filter, pair_list)
     return general(recording, trailing, whiten_filter, pair_list)
 

time: 37.8 us -> 35 us (0.926)
  local copies, waits for them, and re-layouts: 2.63 us -> 0 us
    unnamed x8 -> x0, local copies, waits for them, and re-layouts: 2.63 us -> none
where the time goes in v3:
time: 35 us; the launch traced here: 34.9 us
  Pallas kernels  34.9 us (100%)
    pallas_call x1, Pallas kernels, fused(): pl.pallas_call(functools.partial(spectra_kernel, chan_count, 1.0 / math.s...  31.8 us
    pallas_call x1, Pallas kernels, fused(): pl.pallas_call(slot_kernel, out_shape=jax.ShapeDtypeStruct((1, SLOTS, 1,...  3.09 us

profile of v3, /device:TPU:0, one launch (start us, length us, event | category | flops | bytes accessed | tf_op | source)
XLA Modules:
  0.0 34.9 jit_solution(10844706879698944920)
XLA Ops:
  0.0 31.8 %shard_map.46.crossed = f32[4,2,256,256]{3,2,1,0:T(8,128)} custom-call(bf16[128,1024]{1,0:T(8,128)(2,1)} %rec_ref.1, bf16[128,1024]{1,0:T(8,128)(2,1)} %trail_ref.1, bf16[64,128]{1,0:T(8,128)(2,1)} %bitcast.1), custom_call_target="tpu_custom_call" | custom-call | tf_op jit(solution)/shard_map/pallas_call | solution.py:524
  31.8 3.1 %shard_map.47 = f32[1,4,1,2,256,256]{5,4,3,2,1,0:T(8,128)} custom-call(s32[1,4]{1,0:T(1,128)} %pairs_ref.1, f32[4,2,256,256]{3,2,1,0:T(8,128)} %shard_map.46.crossed), custom_call_target="tpu_custom_call" | custom-call | tf_op jit(solution)/shard_map/pallas_call | solution.py:549

commit v4 on v3

--- a/solution.py
+++ b/solution.py
@@ -193,9 +193,13 @@
     pl.semaphore_signal(barrier, inc=1, device_id=other_tm, device_id_type=MESH)
     pl.semaphore_signal(barrier, inc=1, device_id=other_core, device_id_type=MESH)
 
-    for distance in range(1, chan_count):
-        peer = {"chan": lax.rem(me + distance, chan_count)}
-        pl.semaphore_signal(barrier, inc=1, device_id=peer, device_id_type=MESH)
+    @pl.when(has_left)
+    def _():
+        pl.semaphore_signal(barrier, inc=1, device_id=left, device_id_type=MESH)
+
+    @pl.when(has_right)
+    def _():
+        pl.semaphore_signal(barrier, inc=1, device_id=right, device_id_type=MESH)
 
     own_copies = [
         pltpu.make_async_copy(rec_ref, samples.at[tm, half(core)], local_sems.at[0]),
@@ -205,7 +209,7 @@
     for copy in own_copies:
         copy.start()
 
-    pl.semaphore_wait(barrier, 1 + chan_count)
+    pl.semaphore_wait(barrier, 2 + has_left.astype(jnp.int32) + has_right.astype(jnp.int32))
 
     def piece_start(which, step):
         return pl.multiple_of(
@@ -238,18 +242,21 @@
     def exists(direction, distance):
         return me - distance >= 0 if direction == 0 else me + distance < chan_count
 
-    def weights_copy(direction, distance):
-        device = {"chan": me + distance if direction == 0 else me - distance}
-        return remote(
-            filt_ref, filters.at[core, me], filter_sems, (direction, distance - 1), device
-        )
-
-    for distance in range(1, chan_count):
-        for direction in range(2):
-
-            @pl.when(exists(1 - direction, distance))
-            def _():
-                weights_copy(direction, distance).start()
+    ahead = (has_right, has_left)
+    furthest = chan_count - 1
+
+    def weights_copy(direction, distance, sem):
+        source = me - distance if direction == 0 else me + distance
+        at = filters.at[core, jnp.clip(source, 0, chan_count - 1)]
+        device = right if direction == 0 else left
+        held = filt_ref if distance == 0 else at
+        return remote(held, at, filter_sems, (direction, sem), device)
+
+    for direction in range(2):
+
+        @pl.when(ahead[direction])
+        def _():
+            weights_copy(direction, 0, 0).start()
 
     first_bin = (tm * 2 + core) * width
     unit = 2.0 * math.pi / window
@@ -288,9 +295,6 @@
 
     for copy in own_copies:
         copy.wait()
-    remote(rec_ref, samples.at[tm, half(other)], core_sems, (0,), other_core).wait_recv()
-    remote(trail_ref, samples.at[2, half(other)], core_sems, (1,), other_core).wait_recv()
-
     def own_rows(block, start, count):
         return pl.ds(pl.multiple_of(rim + block * block_rows + start, piece), count)
 
@@ -309,8 +313,6 @@
 
     def landed(direction, distance, tier):
         return block_copy(direction, distance, tier, distance - 1)
-
-    ahead = (has_right, has_left)
 
     def transform(which, p, tier):
         at = which * rows + piece_start(which, p)
@@ -336,6 +338,11 @@
             def _():
                 outgoing(direction, 0, tier).start()
 
+    def transform_passed(p):
+        theirs = samples.at[1 - tm, piece_in_block(other, p)]
+        remote(theirs, theirs, pass_sems, (p,), other_core).wait_recv()
+        transform(other, p, PIECES + p)
+
     pass_copies = []
     for p in range(PIECES):
         mine = samples.at[1 - tm, piece_in_block(core, p)]
@@ -344,25 +351,49 @@
         passing.start()
         pass_copies.append(passing)
         transform(core, p, p)
-
-    for distance in range(1, chan_count):
-        for direction in range(2):
-
-            @pl.when(exists(direction, distance))
-            def _():
-                at = filters.at[core, me - distance if direction == 0 else me + distance]
-                remote(at, at, filter_sems, (direction, distance - 1), other_core).wait_recv()
-
-    core_copies.append(
-        remote(filters.at[core], filters.at[core], core_sems, (2,), other_core)
-    )
+        if p == 0:
+            remote(rec_ref, samples.at[tm, half(other)], core_sems, (0,), other_core).wait_recv()
+            remote(trail_ref, samples.at[2, half(other)], core_sems, (1,), other_core).wait_recv()
+        else:
+            transform_passed(p - 1)
+        distance = p + 1
+        if distance <= furthest:
+            for direction in range(2):
+
+                @pl.when(exists(direction, distance))
+                def _():
+                    weights_copy(direction, distance, distance - 1).wait_recv()
+
+                if distance < furthest:
+
+                    @pl.when(jnp.logical_and(exists(direction, distance), ahead[direction]))
+                    def _():
+                        weights_copy(direction, distance, distance).start()
+
+    core_copies.append(remote(filters.at[core], filters.at[core], core_sems, (2,), other_core))
     core_copies[-1].start()
-
-    for p in range(PIECES):
-        theirs = samples.at[1 - tm, piece_in_block(other, p)]
-        remote(theirs, theirs, pass_sems, (p,), other_core).wait_recv()
-        transform(other, p, PIECES + p)
-
+    transform_passed(PIECES - 1)
+
+    order = [0]
+    for p in range(1, PIECES):
+        order += [p, PIECES + p - 1]
+    order.append(2 * PIECES - 1)
+
+    def advance(distance, chosen):
+        for tier in chosen:
+            for direction in range(2):
+
+                @pl.when(exists(direction, distance))
+                def _():
+                    landed(direction, distance, tier).wait_recv()
+
+                if distance < furthest:
+
+                    @pl.when(jnp.logical_and(exists(direction, distance), ahead[direction]))
+                    def _():
+                        outgoing(direction, distance, tier).start()
+
+    advance(1, order[:PIECES])
     remote(filters.at[other], filters.at[other], core_sems, (2,), other_core).wait_recv()
 
     def spread(block, carry):
@@ -419,28 +450,14 @@
             whiten(block, 0 if direction == 0 else tile_count - 1)
             cross(block, 2 * distance - 1 + direction)
 
-    furthest = chan_count - 1
     for distance in range(1, chan_count):
-        for tier in range(len(tiers)):
+        if distance == 1:
+            finish_own()
+        else:
+            advance(distance, order[:PIECES])
             for direction in range(2):
-
-                @pl.when(exists(direction, distance))
-                def _():
-                    landed(direction, distance, tier).wait_recv()
-
-                if distance < furthest:
-
-                    @pl.when(jnp.logical_and(exists(direction, distance), ahead[direction]))
-                    def _():
-                        outgoing(direction, distance, tier).start()
-
-            if tier == PIECES:
-                if distance == 1:
-                    finish_own()
-                else:
-                    for direction in range(2):
-                        finish(direction, distance - 1)
-
+                finish(direction, distance - 1)
+        advance(distance, order[PIECES:])
         for direction in range(2):
 
             @pl.when(exists(direction, distance))
@@ -455,12 +472,12 @@
     for copy in span_copies + core_copies + pass_copies:
         copy.wait_send()
 
-    for distance in range(1, chan_count):
+    for distance in range(furthest):
         for direction in range(2):
 
-            @pl.when(exists(1 - direction, distance))
+            @pl.when(jnp.logical_and(exists(direction, distance), ahead[direction]))
             def _():
-                weights_copy(direction, distance).wait_send()
+                weights_copy(direction, distance, distance).wait_send()
 
     for distance in range(furthest):
         for tier in range(len(tiers)):

time: 35 us -> 35 us (level)
  no operation moved by 1% of the time
where the time goes in v4:
time: 35 us; the launch traced here: 34.9 us
  Pallas kernels  34.9 us (100%)
    pallas_call x1, Pallas kernels, fused(): pl.pallas_call(functools.partial(spectra_kernel, chan_count, 1.0 / math.s...  31.8 us
    pallas_call x1, Pallas kernels, fused(): pl.pallas_call(slot_kernel, out_shape=jax.ShapeDtypeStruct((1, SLOTS, 1,...  3.09 us

profile of v4, /device:TPU:0, one launch (start us, length us, event | category | flops | bytes accessed | tf_op | source)
XLA Modules:
  0.0 34.9 jit_solution(17640743981777421545)
XLA Ops:
  0.0 31.8 %shard_map.46.crossed = f32[4,2,256,256]{3,2,1,0:T(8,128)} custom-call(bf16[128,1024]{1,0:T(8,128)(2,1)} %rec_ref.1, bf16[128,1024]{1,0:T(8,128)(2,1)} %trail_ref.1, bf16[64,128]{1,0:T(8,128)(2,1)} %bitcast.1), custom_call_target="tpu_custom_call" | custom-call | tf_op jit(solution)/shard_map/pallas_call | solution.py:541
  31.8 3.1 %shard_map.47 = f32[1,4,1,2,256,256]{5,4,3,2,1,0:T(8,128)} custom-call(s32[1,4]{1,0:T(1,128)} %pairs_ref.1, f32[4,2,256,256]{3,2,1,0:T(8,128)} %shard_map.46.crossed), custom_call_target="tpu_custom_call" | custom-call | tf_op jit(solution)/shard_map/pallas_call | solution.py:566
